TPU v7x, 32 devices: a whole 2x2x4 slice. The times are simulated.
32 devices in a mesh: gx: 8 (over y, x, core), gy: 4 (over z).
Axes of the slice: x: 2, y: 2, z: 4, core: 2. Of those that a mesh axis runs over, the one named last changes fastest.
Arguments:
- blocks: bfloat16 [8, 4, 128, 128, 128], P('gx', 'gy'), may hold values from -0.1875 to 0.1875
- pattern: int32 [8, 4, 128], P('gx', 'gy'), may hold values from 0 to 255, as said below
- local_src: bfloat16 [8, 4, 2, 32, 2048], P('gx', 'gy'), may hold values from -4 to 4
- owner: int32 [2, 32], replicated, may hold values from 0 to 31
Outputs:
- sweep_out: bfloat16 [8, 4, 2, 32, 2048], P('gx', 'gy')
Inputs may be any that keep to these rules, and one draw needn't show every extreme that they name: `pattern`: the 128 values of one cell are distinct.
All inputs are finite; a program needn't handle non-finite values.
Results may differ from a plain program's by a relative error of at most 0.019.
Values may be sent and summed in bfloat16 or wider, within the bound.
A program may use at most 64 MiB of HBM per device.

v0:
```python
import functools

import jax
import jax.numpy as jnp
from jax import lax
from jax.experimental import pallas as pl
from jax.experimental.pallas import tpu as pltpu
from jax.sharding import PartitionSpec as P

MESH = pl.DeviceIdType.MESH
GROUPS = 2
CHUNK = 256
PARTS = 4
HEAD = 2
UNROLL = 16


def kernel(
    dims,
    blocks_hbm,
    pattern_hbm,
    src_hbm,
    owner_hbm,
    out_ref,
    blk,
    pat_v,
    own_v,
    src_v,
    inv_v,
    inv_s,
    acc,
    inbuf,
    outbuf,
    load_sem,
    send_sem,
    recv_sem,
):
    nx, ny, nnz, order, rows, width = dims
    trace = width // 2
    nblk = width // order
    group = rows // GROUPS
    per_dir = trace // CHUNK
    sub = CHUNK // order
    me_x = lax.axis_index("gx")
    me_y = lax.axis_index("gy")
    has = (me_x > 0, me_y > 0)
    sends = (me_x < nx - 1, me_y < ny - 1)
    before = ((me_x - 1, me_y), (me_x, me_y - 1))
    after = ((me_x + 1, me_y), (me_x, me_y + 1))

    barrier = pltpu.get_barrier_semaphore()
    for d in range(2):

        @pl.when(has[d])
        def _():
            pl.semaphore_signal(barrier, inc=1, device_id=before[d], device_id_type=MESH)

    pat_copy = pltpu.make_async_copy(pattern_hbm, pat_v, load_sem.at[0])
    own_copy = pltpu.make_async_copy(owner_hbm, own_v, load_sem.at[1])
    src_copy = pltpu.make_async_copy(src_hbm, src_v, load_sem.at[2])
    pat_copy.start()
    own_copy.start()
    src_copy.start()
    step = nnz // PARTS
    blk_copies = [
        pltpu.make_async_copy(
            blocks_hbm.at[pl.ds(p * step, step)],
            blk.at[pl.ds(p * step, step)],
            load_sem.at[3 + p],
        )
        for p in range(PARTS)
    ]
    for copy in blk_copies:
        copy.start()
    blk[nnz] = jnp.zeros((order, order), blk.dtype)

    own_copy.wait()
    src_copy.wait()
    cell_id = me_x * ny + me_y
    nbatch, nsource = own_v.shape
    eye = lax.broadcasted_iota(jnp.int32, (nsource, nsource), 0) == lax.broadcasted_iota(
        jnp.int32, (nsource, nsource), 1
    )
    for b in range(nbatch):
        mine = (own_v[b : b + 1, :] == cell_id).astype(jnp.float32)
        mask = jnp.sum(jnp.where(eye, mine, 0.0), axis=1, keepdims=True)
        span = pl.ds(b * nsource, nsource)
        acc[span, :] = src_v[span, :].astype(jnp.float32) * mask

    wanted = sum(s.astype(jnp.int32) for s in sends)

    @pl.when(wanted > 0)
    def _():
        pl.semaphore_wait(barrier, wanted)

    def transfer(g, d, c):
        return pltpu.make_async_remote_copy(
            src_ref=outbuf.at[g, d, c],
            dst_ref=inbuf.at[g, d, c],
            send_sem=send_sem.at[g, d, c],
            recv_sem=recv_sem.at[g, d, c],
            device_id=after[d],
            device_id_type=MESH,
        )

    def weights(o, k):
        rows_of = []
        for b in range(sub):
            parts = []
            for a in range(sub):
                f = (o * sub + a) * nblk + k * sub + b
                parts.append(blk[inv_s[f // nnz, f % nnz]])
            rows_of.append(jnp.concatenate(parts, axis=1))
        return jnp.concatenate(rows_of, axis=0)

    def as_stored(o, k):
        rows_of = []
        for a in range(sub):
            f = (o * sub + a) * nblk + k * sub
            parts = [blk[inv_s[(f + b) // nnz, (f + b) % nnz]] for b in range(sub)]
            rows_of.append(jnp.concatenate(parts, axis=1))
        return jnp.concatenate(rows_of, axis=0)

    def product(g, d, c, outs, stored):
        if stored:
            tall = [as_stored(o, d * per_dir + c) for o in outs]
            return lax.dot_general(
                inbuf[g, d, c],
                jnp.concatenate(tall, axis=0),
                (((1,), (1,)), ((), ())),
                preferred_element_type=jnp.float32,
            )
        wide = [weights(o, d * per_dir + c) for o in outs]
        return jnp.dot(
            inbuf[g, d, c],
            jnp.concatenate(wide, axis=1),
            preferred_element_type=jnp.float32,
        )

    def emit(g, d, c, value):
        o = d * per_dir + c
        result = value.astype(jnp.bfloat16)
        outbuf[g, d, c] = result
        out_ref[pl.ds(g * group, group), pl.ds(o * CHUNK, CHUNK)] = result

        @pl.when(sends[d])
        def _():
            transfer(g, d, c).start()

    def place(g, d, c):
        return (pl.ds(g * group, group), pl.ds((d * per_dir + c) * CHUNK, CHUNK))

    ordered = [(d, c) for c in range(per_dir) for d in range(2)]
    early = me_x + me_y == 1
    any_input = jnp.logical_or(has[0], has[1])

    @pl.when(jnp.logical_not(any_input))
    def _():
        for g in range(GROUPS):
            for d, c in ordered:
                emit(g, d, c, acc[place(g, d, c)])
        pat_copy.wait()
        for copy in blk_copies:
            copy.wait()

    @pl.when(any_input)
    def _():
        pat_copy.wait()
        pat_t = jnp.transpose(jnp.broadcast_to(pat_v[...], (nnz, nnz)))
        lane = lax.broadcasted_iota(jnp.int32, (nnz, nnz), 1)
        which = lax.broadcasted_iota(jnp.int32, (nnz, nnz), 0)
        for h in range(nblk * nblk // nnz):
            hit = jnp.where(pat_t == lane + h * nnz, which, nnz)
            inv_v[h : h + 1, :] = jnp.min(hit, axis=0, keepdims=True)
        inv_copy = pltpu.make_async_copy(inv_v, inv_s, load_sem.at[3 + PARTS])
        inv_copy.start()
        inv_copy.wait()

        for p, copy in enumerate(blk_copies):
            copy.wait()

            def turn(i, carry):
                for u in range(UNROLL):
                    at = p * step + i * UNROLL + u
                    blk[at] = jnp.transpose(blk[at])
                return carry

            @pl.when(jnp.logical_not(early))
            def _():
                lax.fori_loop(0, step // UNROLL, turn, 0)

        def apply(g, dirs, stored):
            for c in range(HEAD):
                for d in dirs:
                    transfer(g, d, c).wait_recv()
                for oc in range(per_dir):
                    both = sum(product(g, d, c, (oc, per_dir + oc), stored) for d in dirs)
                    for od in range(2):
                        at = place(g, od, oc)
                        acc[at] = acc[at] + both[:, od * CHUNK : (od + 1) * CHUNK]
            for c in range(HEAD, per_dir):
                for d in dirs:
                    transfer(g, d, c).wait_recv()
            for oc in range(per_dir):
                both = sum(
                    product(g, d, c, (oc, per_dir + oc), stored)
                    for c in range(HEAD, per_dir)
                    for d in dirs
                )
                for od in range(2):
                    value = acc[place(g, od, oc)] + both[:, od * CHUNK : (od + 1) * CHUNK]
                    emit(g, od, oc, value)

        for dirs in ((0, 1), (0,), (1,)):
            here = [has[d] if d in dirs else jnp.logical_not(has[d]) for d in range(2)]
            for stored in (False, True) if len(dirs) == 1 else (False,):
                when = early if stored else jnp.logical_not(early)

                @pl.when(jnp.logical_and(jnp.logical_and(here[0], here[1]), when))
                def _():
                    for g in range(GROUPS):
                        apply(g, dirs, stored)

    for g in range(GROUPS):
        for d, c in ordered:

            @pl.when(sends[d])
            def _():
                transfer(g, d, c).wait_send()


def body(nx, ny, blocks, pattern, local_src, owner):
    nnz, order = blocks.shape[2], blocks.shape[3]
    nbatch, nsource, width = local_src.shape[2:]
    rows = nbatch * nsource
    nblk = width // order
    per_dir = width // 2 // CHUNK
    group = rows // GROUPS
    dims = (nx, ny, nnz, order, rows, width)
    any_spec = pl.BlockSpec(memory_space=pl.ANY)
    result = pl.pallas_call(
        functools.partial(kernel, dims),
        name="sweep",
        out_shape=pltpu.VMEM((rows, width), jnp.bfloat16),
        in_specs=[any_spec] * 4,
        out_specs=pl.BlockSpec(memory_space=pltpu.VMEM),
        scratch_shapes=[
            pltpu.VMEM((nnz + 1, order, order), jnp.bfloat16),
            pltpu.VMEM((1, nnz), jnp.int32),
            pltpu.VMEM((nbatch, nsource), jnp.int32),
            pltpu.VMEM((rows, width), jnp.bfloat16),
            pltpu.VMEM((nblk * nblk // nnz, nnz), jnp.int32),
            pltpu.SMEM((nblk * nblk // nnz, nnz), jnp.int32),
            pltpu.VMEM((rows, width), jnp.float32),
            pltpu.VMEM((GROUPS, 2, per_dir, group, CHUNK), jnp.bfloat16),
            pltpu.VMEM((GROUPS, 2, per_dir, group, CHUNK), jnp.bfloat16),
            pltpu.SemaphoreType.DMA((4 + PARTS,)),
            pltpu.SemaphoreType.DMA((GROUPS, 2, per_dir)),
            pltpu.SemaphoreType.DMA((GROUPS, 2, per_dir)),
        ],
        compiler_params=pltpu.CompilerParams(collective_id=0, has_side_effects=True),
    )(
        blocks.reshape(nnz, order, order),
        pattern.reshape(1, nnz),
        local_src.reshape(rows, width),
        owner,
    )
    return result.reshape(1, 1, nbatch, nsource, width)


def solution(mesh):
    return jax.shard_map(
        functools.partial(body, mesh.shape["gx"], mesh.shape["gy"]),
        mesh=mesh,
        in_specs=(
            P("gx", "gy", None, None, None),
            P("gx", "gy", None),
            P("gx", "gy", None, None, None),
            P(),
        ),
        out_specs=P("gx", "gy", None, None, None),
        check_vma=False,
    )
```

profile of v0, /device:TPU:31, one launch (start us, length us, event | category | flops | bytes accessed | tf_op | source)
XLA Modules:
  0.0 34.3 jit_solution(8115588348918174595)
XLA Ops:
  0.0 33.6 %sweep.1 = bf16[64,2048]{1,0:T(8,128)(2,1)S(1)} custom-call(bf16[128,128,128]{2,1,0:T(8,128)(2,1)} %bitcast.5, s32[1,128]{1,0:T(1,128)} %bitcast.7, bf16[64,2048]{1,0:T(8,128)(2,1)} %bitcast.6, s32[2,32]{1,0:T(2,128)} %owner_hbm.1), custom_call_target="tpu_custom_call" | custom-call | tf_op jit(solution)/shard_map/sweep/pallas_call | solution.py:241
  33.6 0.7 %copy.6 = bf16[1,1,2,32,2048]{4,3,2,1,0:T(8,128)(2,1)} copy(bf16[1,1,2,32,2048]{4,3,2,1,0:T(8,128)(2,1)S(1)} %bitcast.4) | data formatting | bytes 524288
where the time goes:
time: 34.4 us; the launch traced here: 34.3 us
  Pallas kernels  33.6 us (98%)
  local copies, waits for them, and re-layouts  0.71 us (2%)
    pallas_call x1, Pallas kernels, body(): pl.pallas_call(functools.partial(kernel, dims), name='sweep', out_shape=p...  33.6 us
    unnamed x1, local copies, waits for them, and re-layouts  0.71 us

commit v1 on v0

--- a/solution.py
+++ b/solution.py
@@ -11,8 +11,9 @@
 GROUPS = 2
 CHUNK = 256
 PARTS = 4
+UNROLL = 16
 HEAD = 2
-UNROLL = 16
+LEFT, BOTTOM = 0, 1
 
 
 def kernel(
@@ -31,9 +32,13 @@
     acc,
     inbuf,
     outbuf,
+    relay,
     load_sem,
     send_sem,
     recv_sem,
+    relay_send,
+    relay_recv,
+    onward_sem,
 ):
     nx, ny, nnz, order, rows, width = dims
     trace = width // 2
@@ -48,6 +53,14 @@
     before = ((me_x - 1, me_y), (me_x, me_y - 1))
     after = ((me_x + 1, me_y), (me_x, me_y + 1))
 
+    relayed = nx > 1 and ny > 1
+    origin = jnp.logical_and(me_x == 0, me_y == 0)
+    helper = jnp.logical_and(me_x == 1, me_y == 0)
+    above_origin = jnp.logical_and(me_x == 0, me_y == 1)
+    if relayed:
+        before_y = (jnp.where(above_origin, 1, me_x), me_y - 1)
+        before = (before[0], before_y)
+
     barrier = pltpu.get_barrier_semaphore()
     for d in range(2):
 
@@ -88,6 +101,8 @@
         acc[span, :] = src_v[span, :].astype(jnp.float32) * mask
 
     wanted = sum(s.astype(jnp.int32) for s in sends)
+    if relayed:
+        wanted = wanted + helper.astype(jnp.int32) - origin.astype(jnp.int32)
 
     @pl.when(wanted > 0)
     def _():
@@ -121,15 +136,7 @@
             rows_of.append(jnp.concatenate(parts, axis=1))
         return jnp.concatenate(rows_of, axis=0)
 
-    def product(g, d, c, outs, stored):
-        if stored:
-            tall = [as_stored(o, d * per_dir + c) for o in outs]
-            return lax.dot_general(
-                inbuf[g, d, c],
-                jnp.concatenate(tall, axis=0),
-                (((1,), (1,)), ((), ())),
-                preferred_element_type=jnp.float32,
-            )
+    def product(g, d, c, outs):
         wide = [weights(o, d * per_dir + c) for o in outs]
         return jnp.dot(
             inbuf[g, d, c],
@@ -137,28 +144,69 @@
             preferred_element_type=jnp.float32,
         )
 
-    def emit(g, d, c, value):
-        o = d * per_dir + c
+    def stored_product(c, outs):
+        tall = [as_stored(o, c) for o in outs]
+        return lax.dot_general(
+            jnp.concatenate([inbuf[g, LEFT, c] for g in range(GROUPS)], axis=0),
+            jnp.concatenate(tall, axis=0),
+            (((1,), (1,)), ((), ())),
+            preferred_element_type=jnp.float32,
+        )
+
+    def handed(g, c):
+        return pltpu.make_async_remote_copy(
+            src_ref=outbuf.at[g, BOTTOM, c],
+            dst_ref=relay.at[g, c],
+            send_sem=relay_send.at[g, c],
+            recv_sem=relay_recv.at[g, c],
+            device_id=(me_x + 1, me_y),
+            device_id_type=MESH,
+        )
+
+    def onward(g, c):
+        return pltpu.make_async_remote_copy(
+            src_ref=relay.at[g, c],
+            dst_ref=inbuf.at[g, BOTTOM, c],
+            send_sem=onward_sem.at[g, c],
+            recv_sem=recv_sem.at[g, BOTTOM, c],
+            device_id=(me_x - 1, me_y + 1),
+            device_id_type=MESH,
+        )
+
+    def place(g, d, c):
+        return (pl.ds(g * group, group), pl.ds((d * per_dir + c) * CHUNK, CHUNK))
+
+    def store(g, d, c, value):
         result = value.astype(jnp.bfloat16)
         outbuf[g, d, c] = result
-        out_ref[pl.ds(g * group, group), pl.ds(o * CHUNK, CHUNK)] = result
-
+        out_ref[place(g, d, c)] = result
+
+    def send(g, d, c):
         @pl.when(sends[d])
         def _():
             transfer(g, d, c).start()
 
-    def place(g, d, c):
-        return (pl.ds(g * group, group), pl.ds((d * per_dir + c) * CHUNK, CHUNK))
-
-    ordered = [(d, c) for c in range(per_dir) for d in range(2)]
-    early = me_x + me_y == 1
+    def emit(g, d, c, value):
+        store(g, d, c, value)
+        send(g, d, c)
+
+    pairs = [((LEFT, c), (BOTTOM, c)) for c in range(per_dir)]
+
+    def number(pair):
+        return tuple(d * per_dir + c for d, c in pair)
+
+    ordered = [(d, c) for c in range(per_dir) for d in (BOTTOM, LEFT)]
     any_input = jnp.logical_or(has[0], has[1])
 
     @pl.when(jnp.logical_not(any_input))
     def _():
         for g in range(GROUPS):
             for d, c in ordered:
-                emit(g, d, c, acc[place(g, d, c)])
+                if relayed and d == BOTTOM:
+                    store(g, d, c, acc[place(g, d, c)])
+                    handed(g, c).start()
+                else:
+                    emit(g, d, c, acc[place(g, d, c)])
         pat_copy.wait()
         for copy in blk_copies:
             copy.wait()
@@ -174,6 +222,15 @@
             inv_v[h : h + 1, :] = jnp.min(hit, axis=0, keepdims=True)
         inv_copy = pltpu.make_async_copy(inv_v, inv_s, load_sem.at[3 + PARTS])
         inv_copy.start()
+        if relayed:
+
+            @pl.when(helper)
+            def _():
+                for g in range(GROUPS):
+                    for c in range(per_dir):
+                        handed(g, c).wait_recv()
+                        onward(g, c).start()
+
         inv_copy.wait()
 
         for p, copy in enumerate(blk_copies):
@@ -185,48 +242,76 @@
                     blk[at] = jnp.transpose(blk[at])
                 return carry
 
-            @pl.when(jnp.logical_not(early))
+            @pl.when(jnp.logical_not(helper))
             def _():
                 lax.fori_loop(0, step // UNROLL, turn, 0)
 
-        def apply(g, dirs, stored):
+        def gather(g, d, c):
+            transfer(g, d, c).wait_recv()
+            for pair in pairs:
+                both = product(g, d, c, number(pair))
+                for n, (od, oc) in enumerate(pair):
+                    at = place(g, od, oc)
+                    acc[at] = acc[at] + both[:, n * CHUNK : (n + 1) * CHUNK]
+
+        def apply(g, dirs):
+            for d in dirs[:-1]:
+                for c in range(per_dir):
+                    gather(g, d, c)
+            d = dirs[-1]
             for c in range(HEAD):
-                for d in dirs:
-                    transfer(g, d, c).wait_recv()
-                for oc in range(per_dir):
-                    both = sum(product(g, d, c, (oc, per_dir + oc), stored) for d in dirs)
-                    for od in range(2):
-                        at = place(g, od, oc)
-                        acc[at] = acc[at] + both[:, od * CHUNK : (od + 1) * CHUNK]
+                gather(g, d, c)
             for c in range(HEAD, per_dir):
-                for d in dirs:
-                    transfer(g, d, c).wait_recv()
-            for oc in range(per_dir):
-                both = sum(
-                    product(g, d, c, (oc, per_dir + oc), stored)
-                    for c in range(HEAD, per_dir)
-                    for d in dirs
-                )
-                for od in range(2):
-                    value = acc[place(g, od, oc)] + both[:, od * CHUNK : (od + 1) * CHUNK]
+                transfer(g, d, c).wait_recv()
+            for pair in pairs:
+                both = sum(product(g, d, c, number(pair)) for c in range(HEAD, per_dir))
+                for n, (od, oc) in enumerate(pair):
+                    value = acc[place(g, od, oc)] + both[:, n * CHUNK : (n + 1) * CHUNK]
                     emit(g, od, oc, value)
 
-        for dirs in ((0, 1), (0,), (1,)):
+        for dirs in ((BOTTOM, LEFT), (LEFT,), (BOTTOM,)):
             here = [has[d] if d in dirs else jnp.logical_not(has[d]) for d in range(2)]
-            for stored in (False, True) if len(dirs) == 1 else (False,):
-                when = early if stored else jnp.logical_not(early)
-
-                @pl.when(jnp.logical_and(jnp.logical_and(here[0], here[1]), when))
-                def _():
-                    for g in range(GROUPS):
-                        apply(g, dirs, stored)
+            here = jnp.logical_and(jnp.logical_and(here[0], here[1]), jnp.logical_not(helper))
+
+            @pl.when(here)
+            def _():
+                for g in range(GROUPS):
+                    apply(g, dirs)
+
+        @pl.when(helper)
+        def _():
+            for g in range(GROUPS):
+                for c in range(per_dir):
+                    transfer(g, LEFT, c).wait_recv()
+            for pair in [((d, c), (d, c + 1)) for d in range(2) for c in range(0, per_dir, 2)]:
+                both = sum(stored_product(c, number(pair)) for c in range(per_dir))
+                for g in range(GROUPS):
+                    for n, (od, oc) in enumerate(pair):
+                        part = both[g * group : (g + 1) * group, n * CHUNK : (n + 1) * CHUNK]
+                        emit(g, od, oc, acc[place(g, od, oc)] + part)
 
     for g in range(GROUPS):
-        for d, c in ordered:
-
-            @pl.when(sends[d])
-            def _():
-                transfer(g, d, c).wait_send()
+        for d in (LEFT, BOTTOM):
+            for c in range(per_dir):
+                if relayed and d == BOTTOM:
+
+                    @pl.when(jnp.logical_and(sends[d], jnp.logical_not(origin)))
+                    def _():
+                        transfer(g, d, c).wait_send()
+
+                    @pl.when(origin)
+                    def _():
+                        handed(g, c).wait_send()
+
+                    @pl.when(helper)
+                    def _():
+                        onward(g, c).wait_send()
+
+                else:
+
+                    @pl.when(sends[d])
+                    def _():
+                        transfer(g, d, c).wait_send()
 
 
 def body(nx, ny, blocks, pattern, local_src, owner):
@@ -254,9 +339,13 @@
             pltpu.VMEM((rows, width), jnp.float32),
             pltpu.VMEM((GROUPS, 2, per_dir, group, CHUNK), jnp.bfloat16),
             pltpu.VMEM((GROUPS, 2, per_dir, group, CHUNK), jnp.bfloat16),
+            pltpu.VMEM((GROUPS, per_dir, group, CHUNK), jnp.bfloat16),
             pltpu.SemaphoreType.DMA((4 + PARTS,)),
             pltpu.SemaphoreType.DMA((GROUPS, 2, per_dir)),
             pltpu.SemaphoreType.DMA((GROUPS, 2, per_dir)),
+            pltpu.SemaphoreType.DMA((GROUPS, per_dir)),
+            pltpu.SemaphoreType.DMA((GROUPS, per_dir)),
+            pltpu.SemaphoreType.DMA((GROUPS, per_dir)),
         ],
         compiler_params=pltpu.CompilerParams(collective_id=0, has_side_effects=True),
     )(

time: 34.4 us -> 32.5 us (0.945)
  Pallas kernels: 33.6 us -> 31.6 us
    pallas_call x1, Pallas kernels: 33.6 us -> 31.6 us  [body(): pl.pallas_call(functools.partial(kernel, dims), name='sweep', out_shape=p...]
where the time goes in v1:
time: 32.5 us; the launch traced here: 32.3 us
  Pallas kernels  31.6 us (97%)
  local copies, waits for them, and re-layouts  0.71 us (2%)
    pallas_call x1, Pallas kernels, body(): pl.pallas_call(functools.partial(kernel, dims), name='sweep', out_shape=p...  31.6 us
    unnamed x1, local copies, waits for them, and re-layouts  0.71 us

profile of v1, /device:TPU:31, one launch (start us, length us, event | category | flops | bytes accessed | tf_op | source)
XLA Modules:
  0.0 32.3 jit_solution(15822098241001369418)
XLA Ops:
  0.0 31.6 %sweep.1 = bf16[64,2048]{1,0:T(8,128)(2,1)S(1)} custom-call(bf16[128,128,128]{2,1,0:T(8,128)(2,1)} %bitcast.5, s32[1,128]{1,0:T(1,128)} %bitcast.7, bf16[64,2048]{1,0:T(8,128)(2,1)} %bitcast.6, s32[2,32]{1,0:T(2,128)} %owner_hbm.1), custom_call_target="tpu_custom_call" | custom-call | tf_op jit(solution)/shard_map/sweep/pallas_call | solution.py:326
  31.6 0.7 %copy.6 = bf16[1,1,2,32,2048]{4,3,2,1,0:T(8,128)(2,1)} copy(bf16[1,1,2,32,2048]{4,3,2,1,0:T(8,128)(2,1)S(1)} %bitcast.4) | data formatting | bytes 524288

commit v2 on v1

--- a/solution.py
+++ b/solution.py
@@ -144,10 +144,19 @@
             preferred_element_type=jnp.float32,
         )
 
+    def whole(d, c):
+        return jnp.concatenate([inbuf[g, d, c] for g in range(GROUPS)], axis=0)
+
+    def whole_product(d, c, outs):
+        wide = [weights(o, d * per_dir + c) for o in outs]
+        return jnp.dot(
+            whole(d, c), jnp.concatenate(wide, axis=1), preferred_element_type=jnp.float32
+        )
+
     def stored_product(c, outs):
         tall = [as_stored(o, c) for o in outs]
         return lax.dot_general(
-            jnp.concatenate([inbuf[g, LEFT, c] for g in range(GROUPS)], axis=0),
+            whole(LEFT, c),
             jnp.concatenate(tall, axis=0),
             (((1,), (1,)), ((), ())),
             preferred_element_type=jnp.float32,
@@ -191,6 +200,9 @@
         send(g, d, c)
 
     pairs = [((LEFT, c), (BOTTOM, c)) for c in range(per_dir)]
+    sideways, upwards = (
+        [((d, c), (d, c + 1)) for c in range(0, per_dir, 2)] for d in (LEFT, BOTTOM)
+    )
 
     def number(pair):
         return tuple(d * per_dir + c for d, c in pair)
@@ -246,44 +258,101 @@
             def _():
                 lax.fori_loop(0, step // UNROLL, turn, 0)
 
-        def gather(g, d, c):
+        def gather(g, d, c, outs):
             transfer(g, d, c).wait_recv()
-            for pair in pairs:
+            for pair in outs:
                 both = product(g, d, c, number(pair))
                 for n, (od, oc) in enumerate(pair):
                     at = place(g, od, oc)
                     acc[at] = acc[at] + both[:, n * CHUNK : (n + 1) * CHUNK]
 
-        def apply(g, dirs):
-            for d in dirs[:-1]:
-                for c in range(per_dir):
-                    gather(g, d, c)
-            d = dirs[-1]
-            for c in range(HEAD):
-                gather(g, d, c)
-            for c in range(HEAD, per_dir):
+        def finish(g, last, outs):
+            for d, c in last:
                 transfer(g, d, c).wait_recv()
-            for pair in pairs:
-                both = sum(product(g, d, c, number(pair)) for c in range(HEAD, per_dir))
+            for pair in outs:
+                both = sum(product(g, d, c, number(pair)) for d, c in last)
                 for n, (od, oc) in enumerate(pair):
                     value = acc[place(g, od, oc)] + both[:, n * CHUNK : (n + 1) * CHUNK]
                     emit(g, od, oc, value)
 
-        for dirs in ((BOTTOM, LEFT), (LEFT,), (BOTTOM,)):
+        def split(dirs):
+            early = [(d, c) for d in dirs[:-1] for c in range(per_dir)]
+            early += [(dirs[-1], c) for c in range(HEAD)]
+            return early, [(dirs[-1], c) for c in range(HEAD, per_dir)]
+
+        def anywhere(dirs):
+            early, last = split(dirs)
+            for g in range(GROUPS):
+                for d, c in early:
+                    gather(g, d, c, pairs)
+                finish(g, last, pairs)
+
+        def top_row(dirs):
+            early, last = split(dirs)
+            for g in range(GROUPS):
+                for d, c in early:
+                    gather(g, d, c, sideways)
+                finish(g, last, sideways)
+            for pair in upwards:
+                both = sum(whole_product(d, c, number(pair)) for d, c in early + last)
+                for n, (od, oc) in enumerate(pair):
+                    at = (slice(None), pl.ds((od * per_dir + oc) * CHUNK, CHUNK))
+                    value = acc[at] + both[:, n * CHUNK : (n + 1) * CHUNK]
+                    out_ref[at] = value.astype(jnp.bfloat16)
+
+        def across(pair):
+            return [
+                (slice(None), pl.ds((od * per_dir + oc) * CHUNK, CHUNK)) for od, oc in pair
+            ]
+
+        def last_cell(dirs):
+            early, last = split(dirs)
+            for g in range(GROUPS):
+                for d, c in early:
+                    if d == dirs[0]:
+                        gather(g, d, c, pairs)
+            for d, c in early:
+                if d != dirs[0]:
+                    for g in range(GROUPS):
+                        transfer(g, d, c).wait_recv()
+                    for pair in pairs:
+                        both = whole_product(d, c, number(pair))
+                        for n, at in enumerate(across(pair)):
+                            acc[at] = acc[at] + both[:, n * CHUNK : (n + 1) * CHUNK]
+            for d, c in last:
+                for g in range(GROUPS):
+                    transfer(g, d, c).wait_recv()
+            for pair in pairs:
+                both = sum(whole_product(d, c, number(pair)) for d, c in last)
+                for n, at in enumerate(across(pair)):
+                    value = acc[at] + both[:, n * CHUNK : (n + 1) * CHUNK]
+                    out_ref[at] = value.astype(jnp.bfloat16)
+
+        top = jnp.logical_and(has[BOTTOM], jnp.logical_not(sends[BOTTOM]))
+        end = jnp.logical_and(jnp.logical_and(top, has[LEFT]), jnp.logical_not(sends[LEFT]))
+        below = jnp.logical_not(top)
+        plans = (
+            (below, (BOTTOM, LEFT), anywhere),
+            (below, (LEFT,), anywhere),
+            (below, (BOTTOM,), anywhere),
+            (jnp.logical_and(top, jnp.logical_not(end)), (BOTTOM, LEFT), top_row),
+            (top, (BOTTOM,), top_row),
+            (end, (BOTTOM, LEFT), last_cell),
+        )
+        for where, dirs, plan in plans:
             here = [has[d] if d in dirs else jnp.logical_not(has[d]) for d in range(2)]
             here = jnp.logical_and(jnp.logical_and(here[0], here[1]), jnp.logical_not(helper))
 
-            @pl.when(here)
+            @pl.when(jnp.logical_and(here, where))
             def _():
-                for g in range(GROUPS):
-                    apply(g, dirs)
+                plan(dirs)
 
         @pl.when(helper)
         def _():
             for g in range(GROUPS):
                 for c in range(per_dir):
                     transfer(g, LEFT, c).wait_recv()
-            for pair in [((d, c), (d, c + 1)) for d in range(2) for c in range(0, per_dir, 2)]:
+            for pair in sideways + upwards:
                 both = sum(stored_product(c, number(pair)) for c in range(per_dir))
                 for g in range(GROUPS):
                     for n, (od, oc) in enumerate(pair):

time: 32.5 us -> 31.8 us (0.978)
  Pallas kernels: 31.6 us -> 30.9 us
    pallas_call x1, Pallas kernels: 31.6 us -> 30.9 us  [body(): pl.pallas_call(functools.partial(kernel, dims), name='sweep', out_shape=p...]
where the time goes in v2:
time: 31.8 us; the launch traced here: 31.6 us
  Pallas kernels  30.9 us (97%)
  local copies, waits for them, and re-layouts  0.71 us (2%)
    pallas_call x1, Pallas kernels, body(): pl.pallas_call(functools.partial(kernel, dims), name='sweep', out_shape=p...  30.9 us
    unnamed x1, local copies, waits for them, and re-layouts  0.71 us

profile of v2, /device:TPU:31, one launch (start us, length us, event | category | flops | bytes accessed | tf_op | source)
XLA Modules:
  0.0 31.6 jit_solution(16207406183292005811)
XLA Ops:
  0.0 30.9 %sweep.1 = bf16[64,2048]{1,0:T(8,128)(2,1)S(1)} custom-call(bf16[128,128,128]{2,1,0:T(8,128)(2,1)} %bitcast.5, s32[1,128]{1,0:T(1,128)} %bitcast.7, bf16[64,2048]{1,0:T(8,128)(2,1)} %bitcast.6, s32[2,32]{1,0:T(2,128)} %owner_hbm.1), custom_call_target="tpu_custom_call" | custom-call | tf_op jit(solution)/shard_map/sweep/pallas_call | solution.py:395
  30.9 0.7 %copy.6 = bf16[1,1,2,32,2048]{4,3,2,1,0:T(8,128)(2,1)} copy(bf16[1,1,2,32,2048]{4,3,2,1,0:T(8,128)(2,1)S(1)} %bitcast.4) | data formatting | bytes 524288

commit v3 on v2

--- a/solution.py
+++ b/solution.py
@@ -87,6 +87,20 @@
         copy.start()
     blk[nnz] = jnp.zeros((order, order), blk.dtype)
 
+    any_input = jnp.logical_or(has[0], has[1])
+    inv_copy = pltpu.make_async_copy(inv_v, inv_s, load_sem.at[3 + PARTS])
+
+    @pl.when(any_input)
+    def _():
+        pat_copy.wait()
+        pat_t = jnp.transpose(jnp.broadcast_to(pat_v[...], (nnz, nnz)))
+        lane = lax.broadcasted_iota(jnp.int32, (nnz, nnz), 1)
+        which = lax.broadcasted_iota(jnp.int32, (nnz, nnz), 0)
+        for h in range(nblk * nblk // nnz):
+            hit = jnp.where(pat_t == lane + h * nnz, which, nnz)
+            inv_v[h : h + 1, :] = jnp.min(hit, axis=0, keepdims=True)
+        inv_copy.start()
+
     own_copy.wait()
     src_copy.wait()
     cell_id = me_x * ny + me_y
@@ -100,6 +114,19 @@
         span = pl.ds(b * nsource, nsource)
         acc[span, :] = src_v[span, :].astype(jnp.float32) * mask
 
+    @pl.when(jnp.logical_and(any_input, jnp.logical_not(helper)))
+    def _():
+        for p, copy in enumerate(blk_copies):
+            copy.wait()
+
+            def turn(i, carry):
+                for u in range(UNROLL):
+                    at = p * step + i * UNROLL + u
+                    blk[at] = jnp.transpose(blk[at])
+                return carry
+
+            lax.fori_loop(0, step // UNROLL, turn, 0)
+
     wanted = sum(s.astype(jnp.int32) for s in sends)
     if relayed:
         wanted = wanted + helper.astype(jnp.int32) - origin.astype(jnp.int32)
@@ -208,8 +235,6 @@
         return tuple(d * per_dir + c for d, c in pair)
 
     ordered = [(d, c) for c in range(per_dir) for d in (BOTTOM, LEFT)]
-    any_input = jnp.logical_or(has[0], has[1])
-
     @pl.when(jnp.logical_not(any_input))
     def _():
         for g in range(GROUPS):
@@ -225,15 +250,6 @@
 
     @pl.when(any_input)
     def _():
-        pat_copy.wait()
-        pat_t = jnp.transpose(jnp.broadcast_to(pat_v[...], (nnz, nnz)))
-        lane = lax.broadcasted_iota(jnp.int32, (nnz, nnz), 1)
-        which = lax.broadcasted_iota(jnp.int32, (nnz, nnz), 0)
-        for h in range(nblk * nblk // nnz):
-            hit = jnp.where(pat_t == lane + h * nnz, which, nnz)
-            inv_v[h : h + 1, :] = jnp.min(hit, axis=0, keepdims=True)
-        inv_copy = pltpu.make_async_copy(inv_v, inv_s, load_sem.at[3 + PARTS])
-        inv_copy.start()
         if relayed:
 
             @pl.when(helper)
@@ -243,20 +259,13 @@
                         handed(g, c).wait_recv()
                         onward(g, c).start()
 
+        @pl.when(helper)
+        def _():
+            for copy in blk_copies:
+                copy.wait()
+
         inv_copy.wait()
 
-        for p, copy in enumerate(blk_copies):
-            copy.wait()
-
-            def turn(i, carry):
-                for u in range(UNROLL):
-                    at = p * step + i * UNROLL + u
-                    blk[at] = jnp.transpose(blk[at])
-                return carry
-
-            @pl.when(jnp.logical_not(helper))
-            def _():
-                lax.fori_loop(0, step // UNROLL, turn, 0)
 
         def gather(g, d, c, outs):
             transfer(g, d, c).wait_recv()
@@ -289,6 +298,7 @@
 
         def top_row(dirs):
             early, last = split(dirs)
+            early, last = early + last[:-1], last[-1:]
             for g in range(GROUPS):
                 for d, c in early:
                     gather(g, d, c, sideways)

time: 31.8 us -> 31.2 us (0.981)
  Pallas kernels: 30.9 us -> 30.3 us
    pallas_call x1, Pallas kernels: 30.9 us -> 30.3 us  [body(): pl.pallas_call(functools.partial(kernel, dims), name='sweep', out_shape=p...]
where the time goes in v3:
time: 31.2 us; the launch traced here: 31 us
  Pallas kernels  30.3 us (97%)
  local copies, waits for them, and re-layouts  0.71 us (2%)
    pallas_call x1, Pallas kernels, body(): pl.pallas_call(functools.partial(kernel, dims), name='sweep', out_shape=p...  30.3 us
    unnamed x1, local copies, waits for them, and re-layouts  0.71 us

profile of v3, /device:TPU:31, one launch (start us, length us, event | category | flops | bytes accessed | tf_op | source)
XLA Modules:
  0.0 31.0 jit_solution(11912517266286456943)
XLA Ops:
  0.0 30.3 %sweep.1 = bf16[64,2048]{1,0:T(8,128)(2,1)S(1)} custom-call(bf16[128,128,128]{2,1,0:T(8,128)(2,1)} %bitcast.5, s32[1,128]{1,0:T(1,128)} %bitcast.7, bf16[64,2048]{1,0:T(8,128)(2,1)} %bitcast.6, s32[2,32]{1,0:T(2,128)} %owner_hbm.1), custom_call_target="tpu_custom_call" | custom-call | tf_op jit(solution)/shard_map/sweep/pallas_call | solution.py:405
  30.3 0.7 %copy.6 = bf16[1,1,2,32,2048]{4,3,2,1,0:T(8,128)(2,1)} copy(bf16[1,1,2,32,2048]{4,3,2,1,0:T(8,128)(2,1)S(1)} %bitcast.4) | data formatting | bytes 524288

commit v4 on v3

--- a/solution.py
+++ b/solution.py
@@ -317,6 +317,7 @@
 
         def last_cell(dirs):
             early, last = split(dirs)
+            early, last = early + last[:-1], last[-1:]
             for g in range(GROUPS):
                 for d, c in early:
                     if d == dirs[0]:

time: 31.2 us -> 31.2 us (level)
  no operation moved by 1% of the time
where the time goes in v4:
time: 31.2 us; the launch traced here: 31.1 us
  Pallas kernels  30.3 us (97%)
  local copies, waits for them, and re-layouts  0.71 us (2%)
    pallas_call x1, Pallas kernels, body(): pl.pallas_call(functools.partial(kernel, dims), name='sweep', out_shape=p...  30.3 us
    unnamed x1, local copies, waits for them, and re-layouts  0.71 us

profile of v4, /device:TPU:31, one launch (start us, length us, event | category | flops | bytes accessed | tf_op | source)
XLA Modules:
  0.0 31.1 jit_solution(7061121115826941159)
XLA Ops:
  0.0 30.3 %sweep.1 = bf16[64,2048]{1,0:T(8,128)(2,1)S(1)} custom-call(bf16[128,128,128]{2,1,0:T(8,128)(2,1)} %bitcast.5, s32[1,128]{1,0:T(1,128)} %bitcast.7, bf16[64,2048]{1,0:T(8,128)(2,1)} %bitcast.6, s32[2,32]{1,0:T(2,128)} %owner_hbm.1), custom_call_target="tpu_custom_call" | custom-call | tf_op jit(solution)/shard_map/sweep/pallas_call | solution.py:406
  30.3 0.7 %copy.6 = bf16[1,1,2,32,2048]{4,3,2,1,0:T(8,128)(2,1)} copy(bf16[1,1,2,32,2048]{4,3,2,1,0:T(8,128)(2,1)S(1)} %bitcast.4) | data formatting | bytes 524288
